TPU v7x, 32 devices: a whole 2x2x4 slice. The times are simulated.
32 devices in a mesh: tm: 8 (over z, core), net: 4 (over y, x).
Axes of the slice: x: 2, y: 2, z: 4, core: 2. Of those that a mesh axis runs over, the one named last changes fastest.
Arguments:
- ptdf: bfloat16 [16384, 4096], P('net'), may hold values from -0.09375 to 0.09375
- demand: float32 [4096, 512], P('net', 'tm'), may hold values from 0 to 2
- generation: float32 [4096, 512], P('net', 'tm'), may hold values from 0 to 2
- cost: float32 [4096, 512], P('net', 'tm'), may hold values from 0.2 to 4
- gen_cap: float32 [4096], P('net'), may hold values from 0.5 to 4
- storage: float32 [2048, 512], P('net', 'tm'), may hold values from -3 to 3
- wear: float32 [2048], P('net'), may hold values from 0.1 to 2
- initial_charge: float32 [2048], P('net'), may hold values from 0 to 2
- leakage: float32 [2048], P('net'), may hold values from 0.0005859375 to 0.05
- line_dual: float32 [16384, 512], P('net', 'tm'), may hold values from -3 to 3
- line_index: int32 [16384], P('net'), may hold values from 0 to 4095
- rating: float32 [4096], replicated, may hold values from 0.3 to 3
- storage_bus: int32 [2048], replicated, may hold values from 0 to 4095
- balance_dual: float32 [512], P('tm'), may hold values from -4 to 4
- hour_block: int32 [512], P('tm'), may hold values from 0 to 23
- block_price: float32 [24], replicated, may hold values from -4 to 4
Outputs:
- generation_next: float32 [4096, 512], P('net', 'tm')
- storage_next: float32 [2048, 512], P('net', 'tm')
- charge: float32 [2048, 512], P('net', 'tm')
- line_dual_next: float32 [16384, 512], P('net', 'tm')
- balance_price: float32 [512], P('tm')
All inputs are finite; a program needn't handle non-finite values.
Results may differ from a plain program's by a relative error of at most 0.0028.
Values may be sent and summed in bfloat16 or wider, within the bound.
A program may use at most 128 MiB of HBM per device.

v0:
```python
import jax
import jax.numpy as jnp
from jax import lax
from jax.sharding import PartitionSpec as P

PASSES = 2


STEP = 0.1
BAL = 0.5
STEP_UNIT = 0.2
ETA = 0.0625


def prefix(part, axis, combine, identity):
    place = lax.axis_index(axis)
    gathered = jax.tree.map(lambda a: lax.all_gather(a, axis), part)
    state = jax.tree.map(lambda a, e: jnp.zeros_like(a) + jnp.asarray(e, a.dtype), part, identity)

    def one(hop, state):
        return combine(
            state, jax.tree.map(lambda a: lax.dynamic_index_in_dim(a, hop, 0, False), gathered)
        )

    return lax.fori_loop(0, place, one, state)


def combine_charge(earlier, later):
    return (earlier[0] * later[0], later[0] * earlier[1] + later[1])


def per_device(
    ptdf,
    demand,
    generation,
    cost,
    gen_cap,
    storage,
    wear,
    initial_charge,
    leakage,
    line_dual,
    line_index,
    rating,
    storage_bus,
    balance_dual,
    hour_block,
    block_price,
):
    limit = jnp.take(rating, line_index)[:, None]
    gathered_units = lax.all_gather(storage.astype(jnp.bfloat16), "net", axis=0, tiled=True)
    unit_columns = jnp.take(ptdf, storage_bus, axis=1)
    unit_flow = jnp.dot(unit_columns, gathered_units, preferred_element_type=jnp.float32)
    unit_part = jnp.sum(storage, axis=0)
    dual = line_dual
    price = balance_dual
    rows = generation.shape[0]
    hours = storage.shape[1]
    gen = generation
    buses = rows * lax.axis_size("net")
    for turn in range(PASSES):
        injection = (gen - demand).astype(jnp.bfloat16)
        flows = unit_flow + jnp.dot(
            ptdf,
            lax.all_gather(injection, "net", axis=0, tiled=True),
            preferred_element_type=jnp.float32,
        )
        shifted = flows + dual
        dual = shifted - jnp.clip(shifted, -limit, limit)
        dual_half = dual.astype(jnp.bfloat16)
        pull = lax.psum_scatter(
            lax.dot_general(
                ptdf, dual_half, (((0,), (0,)), ((), ())), preferred_element_type=jnp.float32
            ).astype(jnp.bfloat16),
            "net",
            scatter_dimension=0,
            tiled=True,
        ).astype(jnp.float32)
        trial = jnp.clip(gen - STEP * (cost - price[None, :] + pull), 0.0, gen_cap[:, None])
        bus_sum, unit_total = lax.psum((jnp.sum(trial - demand, axis=0), unit_part), "net")
        mismatch = bus_sum + unit_total
        gen = trial - mismatch[None, :] / buses
        price = price - BAL * mismatch / buses
    blocks = block_price.shape[0]
    hour_price = jnp.sum(
        jnp.where(
            hour_block[:, None] == jnp.arange(blocks, dtype=jnp.int32)[None, :],
            block_price[None, :],
            0.0,
        ),
        axis=1,
    )
    storage_next = jnp.clip(
        storage + STEP_UNIT * (price[None, :] + hour_price[None, :] - wear[:, None] * storage),
        -1.0,
        1.0,
    )
    keep = 1.0 - leakage
    running = -ETA * storage_next
    factor = keep[:, None]
    span = 1
    while span < hours:
        moved = jnp.pad(running[:, :-span], ((0, 0), (span, 0)))
        running = running + factor * moved
        factor = factor * factor
        span = span * 2
    offsets = jnp.arange(1, hours + 1, dtype=jnp.float32)
    growth = jnp.exp(offsets[None, :] * jnp.log(keep)[:, None])
    block_keep = growth[:, -1]
    chained = prefix(
        (block_keep, running[:, -1]),
        "tm",
        combine_charge,
        (jnp.ones_like(block_keep), jnp.zeros_like(block_keep)),
    )
    entering = chained[0] * initial_charge + chained[1]
    charge = growth * entering[:, None] + running
    return (gen, storage_next, charge, dual, price)


def solution(mesh):
    in_specs = (
        P("net", None),
        P("net", "tm"),
        P("net", "tm"),
        P("net", "tm"),
        P("net"),
        P("net", "tm"),
        P("net"),
        P("net"),
        P("net"),
        P("net", "tm"),
        P("net"),
        P(),
        P(),
        P("tm"),
        P("tm"),
        P(),
    )
    out_specs = (P("net", "tm"), P("net", "tm"), P("net", "tm"), P("net", "tm"), P("tm"))
    return jax.shard_map(
        per_device, mesh=mesh, in_specs=in_specs, out_specs=out_specs, check_vma=False
    )
```

profile of v0, /device:TPU:0, one launch (start us, length us, event | category | flops | bytes accessed | tf_op | source)
XLA Modules:
  0.0 335.8 jit_solution(408022187996536155)
XLA Ops:
  7.2 0.0 copy-start
  7.2 0.0 reduce-scatter.3.cloned.1.call-start
  7.2 0.7 fusion.13
  7.9 0.7 compare_and_fusion
  8.6 1.1 fusion.21
  9.7 10.5 %all_gather.15 = bf16[2048,64]{0,1:T(8,128)(2,1)S(1)} all-gather(bf16[512,64]{0,1:T(8,128)(2,1)S(1)} %get-tuple-element.68), channel_id=1, replica_groups=mesh['tm'=8,'net'=4] {'net'}, dimensions={0}, use_global_device_ids=true | all-gather | bytes 327680 | tf_op jit(solution)/shard_map/all_gather | solution.py:51
  20.2 41.2 %copy.23 = bf16[4096,4096]{0,1:T(8,128)(2,1)} copy(bf16[4096,4096]{1,0:T(8,128)(2,1)} %param.18) | data formatting | bytes 67108864 | tf_op args[0]
  61.5 23.0 %gather_fusion.1 = f32[4096]{0:T(1024)S(1)} fusion(f32[4096]{0:T(1024)S(1)} %copy-done, s32[4096]{0:T(1024)S(1)} %fusion.12), kind=kCustom, calls=%fused_computation.1 | custom fusion | bytes 49152 | tf_op jit(solution)/shard_map/jit(_take)/gather | solution.py:50
  84.5 0.0 copy-start.13
  84.6 10.2 %all_gather.16 = bf16[4096,64]{0,1:T(8,128)(2,1)S(1)} all-gather(bf16[1024,64]{0,1:T(8,128)(2,1)S(1)} %subtract_convert_fusion.1), channel_id=1, replica_groups=mesh['tm'=8,'net'=4] {'net'}, dimensions={0}, use_global_device_ids=true | all-gather | bytes 655360 | tf_op jit(solution)/shard_map/all_gather | solution.py:65
  94.8 66.3 %gather_fusion = bf16[2048,4096]{1,0:T(8,128)(2,1)} fusion(bf16[4096,4096]{0,1:T(8,128)(2,1)} %copy.23, s32[2048]{0:T(1024)S(1)} %fusion.13), kind=kCustom, calls=%fused_computation | custom fusion | bytes 33562624 | tf_op jit(solution)/shard_map/jit(_take)/gather | solution.py:52
  161.1 7.5 %fusion = f32[4096,64]{0,1:T(8,128)S(1)} fusion(bf16[2048,64]{0,1:T(8,128)(2,1)S(1)} %all_gather.15, bf16[2048,4096]{1,0:T(8,128)(2,1)} %gather_fusion, pred[2048]{0:T(1024)(128)(4,1)S(1)} %compare_and_fusion), kind=kOutput, calls=%fused_computation.5 | convolution fusion | flops 1082130432 | bytes 18089984 | tf_op jit(solution)/shard_map/dot_general | solution.py:53
  168.6 0.0 copy-start.21
  168.6 15.9 %minimum_subtract_fusion.1 = f32[4096,64]{0,1:T(8,128)S(1)} fusion(f32[4096,64]{0,1:T(8,128)} %param.27, f32[4096,64]{0,1:T(8,128)S(1)} %fusion, bf16[4096,64]{0,1:T(8,128)(2,1)S(1)} %all_gather.16, bf16[4096,4096]{1,0:T(8,128)(2,1)} %param.18, f32[4096]{0:T(1024)S(1)} %get-tuple-element.61, f32[4096]{0:T(1024)S(1)} %get-tuple-element.62), kind=kOutput, calls=%fused_computation.20 | convolution fusion | flops 2148794368 | bytes 37257216 | tf_op jit(solution)/shard_map/dot_general | solution.py:63
  184.6 14.4 %fusion.8 = bf16[4096,64]{0,1:T(8,128)(2,1)} fusion(bf16[4096,4096]{1,0:T(8,128)(2,1)} %param.18, f32[4096,64]{0,1:T(8,128)S(1)} %minimum_subtract_fusion.1), kind=kOutput, calls=%fused_computation.17 | convolution fusion | flops 2148007936 | bytes 35127296 | tf_op jit(solution)/shard_map/dot_general | solution.py:72
  199.1 0.0 reduce-scatter.3.cloned.1.call-update
  199.1 0.0 reduce-scatter.5.cloned.1.call-start
  199.1 25.5 %reduce-scatter.3.cloned.1.call-done = bf16[1024,64]{0,1:T(8,128)(2,1)} async-done(((bf16[4096,64]{0,1:T(8,128)(2,1)}), bf16[1024,64]{0,1:T(8,128)(2,1)}) %reduce-scatter.3.cloned.1.call-update) | async-done | bytes 131088 | tf_op jit(solution)/shard_map/reduce_scatter | solution.py:71
  224.6 1.2 subtract_reduce_fusion.1
  225.8 0.0 copy-start.4
  225.8 8.9 %all-reduce.6 = (f32[64]{0:T(128)S(1)}, f32[64]{0:T(128)S(1)}) all-reduce(f32[64]{0:T(128)S(1)} %get-tuple-element.59, f32[64]{0:T(128)S(1)} %get-tuple-element.67), channel_id=1, replica_groups=mesh['tm'=8,'net'=4] {'net'}, use_global_device_ids=true, to_apply=%region_2.3 | all-reduce | flops 128 | bytes 1024 | tf_op jit(solution)/shard_map/psum | solution.py:80
  234.7 0.5 multiply_subtract_fusion.1
  235.2 0.1 subtract_convert_fusion
  235.3 0.5 copy-done.18
  235.8 10.2 %all_gather.17 = bf16[4096,64]{0,1:T(8,128)(2,1)S(1)} all-gather(bf16[1024,64]{0,1:T(8,128)(2,1)S(1)} %subtract_convert_fusion), channel_id=1, replica_groups=mesh['tm'=8,'net'=4] {'net'}, dimensions={0}, use_global_device_ids=true | all-gather | bytes 655360 | tf_op jit(solution)/shard_map/all_gather | solution.py:65
  246.0 15.7 %minimum_subtract_fusion = f32[4096,64]{0,1:T(8,128)S(1)} fusion(f32[4096,64]{0,1:T(8,128)S(1)} %minimum_subtract_fusion.1, f32[4096,64]{0,1:T(8,128)S(1)} %fusion, bf16[4096,64]{0,1:T(8,128)(2,1)S(1)} %all_gather.17, bf16[4096,4096]{1,0:T(8,128)(2,1)} %param.18, f32[4096]{0:T(1024)} %copy-done.12, f32[4096]{0:T(1024)} %copy-done.13), kind=kOutput, calls=%fused_computation.19 | convolution fusion | flops 2148794368 | bytes 37257216 | tf_op jit(solution)/shard_map/dot_general | solution.py:63
  261.6 0.0 copy-start.2
  261.7 0.0 copy-start.25
  261.7 0.0 copy-start.26
  261.7 0.0 copy-start.5
  261.7 0.0 copy-start.7
  261.8 0.0 copy-start.20
  261.8 14.8 %fusion.9 = bf16[4096,64]{0,1:T(8,128)(2,1)} fusion(bf16[4096,4096]{1,0:T(8,128)(2,1)} %param.18, f32[4096,64]{0,1:T(8,128)S(1)} %minimum_subtract_fusion), kind=kOutput, calls=%fused_computation.18 | convolution fusion | flops 2148007936 | bytes 35127296 | tf_op jit(solution)/shard_map/dot_general | solution.py:72
  276.6 0.0 reduce-scatter.5.cloned.1.call-update
  276.7 0.1 multiply_exponential_fusion
  276.8 12.8 %all-gather = f32[4096,1]{0,1:T(1,128)S(1)} all-gather(f32[512,1]{0,1:T(1,128)S(1)} %slice.36), channel_id=2, replica_groups=mesh['tm'=8,'net'=4] {'tm'}, dimensions={0}, use_global_device_ids=true | all-gather | bytes 18432 | tf_op jit(solution)/shard_map/all_gather | solution.py:17
  289.6 0.5 broadcast.111
  290.2 0.7 reduce.6
  290.9 0.1 select_reduce_fusion
  291.0 10.9 %reduce-scatter.5.cloned.1.call-done = bf16[1024,64]{0,1:T(8,128)(2,1)} async-done(((bf16[4096,64]{0,1:T(8,128)(2,1)}), bf16[1024,64]{0,1:T(8,128)(2,1)}) %reduce-scatter.5.cloned.1.call-update) | async-done | bytes 131088 | tf_op jit(solution)/shard_map/reduce_scatter | solution.py:71
  301.9 1.2 subtract_reduce_fusion
  303.1 9.0 %psum.26 = f32[64]{0:T(128)S(1)} all-reduce(f32[64]{0:T(128)S(1)} %subtract_reduce_fusion), channel_id=1, replica_groups=mesh['tm'=8,'net'=4] {'net'}, use_global_device_ids=true, to_apply=%region_7.8 | all-reduce | flops 64 | bytes 512 | tf_op jit(solution)/shard_map/psum | solution.py:80
  312.0 0.5 fusion.19
  312.5 0.1 broadcast_multiply_fusion
  312.9 12.8 %all-gather.1 = f32[4096,1]{0,1:T(1,128)S(1)} all-gather(f32[512,1]{0,1:T(1,128)S(1)} %slice.43), channel_id=3, replica_groups=mesh['tm'=8,'net'=4] {'tm'}, dimensions={0}, use_global_device_ids=true | all-gather | bytes 18432 | tf_op jit(solution)/shard_map/all_gather | solution.py:17
  325.7 0.7 reduce.7
  326.5 0.8 multiply_add_fusion.1
  327.2 1.8 broadcast_subtract_fusion
  (67 shorter events, 0.4 us)
Async XLA Ops:
  7.2 54.3 %copy-start = (f32[4096]{0:T(1024)S(1)}, f32[4096]{0:T(1024)}, u32[]{:S(2)}) copy-start(f32[4096]{0:T(1024)} %param.29) | copy-start | bytes 49156
  7.2 217.4 %reduce-scatter.3.cloned.1.call-start = ((), (), s32[]{:S(2)}) async-start(), calls=%async_computation.2 | async-start | bytes 655360 | tf_op jit(solution)/shard_map/reduce_scatter | solution.py:71
  20.2 41.2 %copy-start.14 = (s32[4096]{0:T(1024)S(1)}, s32[4096]{0:T(1024)}, u32[]{:S(2)}) copy-start(s32[4096]{0:T(1024)} %param.28) | copy-start | bytes 49156
  20.2 64.3 %copy-start.3 = (f32[1024,64]{0,1:T(8,128)S(1)}, f32[1024,64]{0,1:T(8,128)}, u32[]{:S(2)}) copy-start(f32[1024,64]{0,1:T(8,128)} %param.19) | copy-start | bytes 786436
  20.2 64.3 %copy-start.8 = (f32[1024,64]{0,1:T(8,128)S(1)}, f32[1024,64]{0,1:T(8,128)}, u32[]{:S(2)}) copy-start(f32[1024,64]{0,1:T(8,128)} %param.20) | copy-start | bytes 786436
  84.5 84.0 %copy-start.12 = (f32[4096]{0:T(1024)}, f32[4096]{0:T(1024)S(1)}, u32[]{:S(2)}) copy-start(f32[4096]{0:T(1024)S(1)} %get-tuple-element.61) | copy-start | bytes 49156
  84.5 84.0 %copy-start.13 = (f32[4096]{0:T(1024)}, f32[4096]{0:T(1024)S(1)}, u32[]{:S(2)}) copy-start(f32[4096]{0:T(1024)S(1)} %get-tuple-element.62) | copy-start | bytes 49156
  168.6 56.0 %copy-start.6 = (f32[1024,64]{0,1:T(8,128)S(1)}, f32[1024,64]{0,1:T(8,128)}, u32[]{:S(2)}) copy-start(f32[1024,64]{0,1:T(8,128)} %param.21) | copy-start | bytes 786436
  168.6 56.0 %copy-start.15 = (f32[1024]{0:T(1024)S(1)}, f32[1024]{0:T(1024)}, u32[]{:S(2)}) copy-start(f32[1024]{0:T(1024)} %param.22) | copy-start | bytes 12292
  168.6 56.0 %copy-start.21 = (f32[64]{0:T(128)S(1)}, f32[64]{0:T(128)}, u32[]{:S(2)}) copy-start(f32[64]{0:T(128)} %param.31) | copy-start | bytes 772
  184.6 40.0 %copy-start.9 = (f32[1024,64]{0,1:T(8,128)S(1)}, f32[1024,64]{0,1:T(8,128)}, u32[]{:S(2)}) copy-start(f32[1024,64]{0,1:T(8,128)} %param.20) | copy-start | bytes 786436
  199.1 102.8 %reduce-scatter.5.cloned.1.call-start = ((), (), s32[]{:S(2)}) async-start(), calls=%async_computation.3 | async-start | bytes 655360 | tf_op jit(solution)/shard_map/reduce_scatter | solution.py:71
  225.8 9.6 %copy-start.4 = (f32[1024,64]{0,1:T(8,128)}, f32[1024,64]{0,1:T(8,128)S(1)}, u32[]{:S(2)}) copy-start(f32[1024,64]{0,1:T(8,128)S(1)} %get-tuple-element.60) | copy-start | bytes 786436
  234.7 0.6 copy-start.22
  235.2 0.6 copy-start.18
  246.0 66.6 %copy-start.11 = (f32[512,64]{0,1:T(8,128)S(1)}, f32[512,64]{0,1:T(8,128)}, u32[]{:S(2)}) copy-start(f32[512,64]{0,1:T(8,128)} %param.23) | copy-start | bytes 393220
  246.0 83.0 %copy-start.1 = (f32[4096]{0:T(1024)S(1)}, f32[4096]{0:T(1024)}, u32[]{:S(2)}) copy-start(f32[4096]{0:T(1024)} %param.29) | copy-start | bytes 49156
  261.6 67.3 %copy-start.2 = (f32[4096,64]{0,1:T(8,128)}, f32[4096,64]{0,1:T(8,128)S(1)}, u32[]{:S(2)}) copy-start(f32[4096,64]{0,1:T(8,128)S(1)} %minimum_subtract_fusion) | copy-start | bytes 3145732
  261.7 15.0 %copy-start.25 = (f32[512]{0:T(512)S(1)}, f32[512]{0:T(512)}, u32[]{:S(2)}) copy-start(f32[512]{0:T(512)} %param.26) | copy-start | bytes 6148
  261.7 29.2 %copy-start.26 = (f32[24]{0:T(128)S(1)}, f32[24]{0:T(128)}, u32[]{:S(2)}) copy-start(f32[24]{0:T(128)} %param.33) | copy-start | bytes 292
  261.7 29.2 %copy-start.27 = (s32[64]{0:T(128)S(1)}, s32[64]{0:T(128)}, u32[]{:S(2)}) copy-start(s32[64]{0:T(128)} %param.32) | copy-start | bytes 772
  261.7 40.2 %copy-start.5 = (f32[1024,64]{0,1:T(8,128)S(1)}, f32[1024,64]{0,1:T(8,128)}, u32[]{:S(2)}) copy-start(f32[1024,64]{0,1:T(8,128)} %copy-done.4) | copy-start | bytes 786436
  261.7 40.2 %copy-start.7 = (f32[1024,64]{0,1:T(8,128)S(1)}, f32[1024,64]{0,1:T(8,128)}, u32[]{:S(2)}) copy-start(f32[1024,64]{0,1:T(8,128)} %param.21) | copy-start | bytes 786436
  261.7 40.2 %copy-start.16 = (f32[1024]{0:T(1024)S(1)}, f32[1024]{0:T(1024)}, u32[]{:S(2)}) copy-start(f32[1024]{0:T(1024)} %param.22) | copy-start | bytes 12292
  261.7 40.2 %copy-start.17 = (f32[64]{0:T(128)S(1)}, f32[64]{0:T(128)}, u32[]{:S(2)}) copy-start(f32[64]{0:T(128)} %get-tuple-element.77) | copy-start | bytes 772
  261.7 40.1 %copy-start.19 = (f32[64]{0:T(128)S(1)}, f32[64]{0:T(128)}, u32[]{:S(2)}) copy-start(f32[64]{0:T(128)} %copy-done.18) | copy-start | bytes 772
  261.7 50.3 %copy-start.23 = (f32[64]{0:T(128)S(1)}, f32[64]{0:T(128)}, u32[]{:S(2)}) copy-start(f32[64]{0:T(128)} %copy-done.22) | copy-start | bytes 772
  261.8 50.8 %copy-start.20 = (f32[512]{0:T(512)S(1)}, f32[512]{0:T(512)}, u32[]{:S(2)}) copy-start(f32[512]{0:T(512)} %param.24) | copy-start | bytes 6148
  261.8 64.7 %copy-start.24 = (f32[512]{0:T(512)S(1)}, f32[512]{0:T(512)}, u32[]{:S(2)}) copy-start(f32[512]{0:T(512)} %param.25) | copy-start | bytes 6148
  312.6 16.3 %copy-start.10 = (f32[512,64]{0,1:T(8,128)}, f32[512,64]{0,1:T(8,128)S(1)}, u32[]{:S(2)}) copy-start(f32[512,64]{0,1:T(8,128)S(1)} %get-tuple-element.56) | copy-start | bytes 393220
Sparse Core Ops, SparseCore 0:
  199.2 25.3 reduce-scatter.2
  276.8 25.0 reduce-scatter.4
where the time goes:
time: 339 us; the launch traced here: 336 us
  local copies, waits for them, and re-layouts  132 us (39%)
  blocking collectives  74.3 us (22%)
  matrix products  68.4 us (20%)
  waiting for transfers between devices  36.4 us (11%)
  between operations  14.6 us (4%)
  other arithmetic  10.3 us (3%)
    gather x1, local copies, waits for them, and re-layouts, per_device(): unit_columns = jnp.take(ptdf, storage_bus, axis=1)  66.3 us
    unnamed x57, local copies, waits for them, and re-layouts  41.8 us
    reduce_scatter x2, waiting for transfers between devices, per_device(): lax.psum_scatter(lax.dot_general(ptdf, dual_half, (((0,), (0,)), ((), ())...  36.3 us
    dot_general x2, matrix products, per_device(): jnp.dot(ptdf, lax.all_gather(injection, 'net', axis=0, tiled=True), prefe...  31.6 us
    dot_general x2, matrix products, per_device(): lax.dot_general(ptdf, dual_half, (((0,), (0,)), ((), ())), preferred_elem...  29.3 us
    all_gather x2, blocking collectives, prefix(): gathered = jax.tree.map(lambda a: lax.all_gather(a, axis), part)  25.6 us
    gather x1, local copies, waits for them, and re-layouts, per_device(): limit = jnp.take(rating, line_index)[:, None]  23 us
    all_gather x2, blocking collectives, per_device(): lax.all_gather(injection, 'net', axis=0, tiled=True)  20.3 us
  transfers between devices with their start and end apart: 2, of which 2 were waited for; matrix products, arithmetic and copies ran while one was open for 0% of the time, Pallas kernels for 0%

commit v1 on v0

v1 whole, which is shorter than its diff:
```python
import functools

import jax
import jax.numpy as jnp
from jax import lax
from jax.experimental import pallas as pl
from jax.experimental.pallas import tpu as pltpu
from jax.sharding import PartitionSpec as P

PASSES = 2
STEP = 0.1
BAL = 0.5
STEP_UNIT = 0.2
ETA = 0.0625
MESH = pl.DeviceIdType.MESH
NT = (((1,), (1,)), ((), ()))
NN = (((1,), (0,)), ((), ()))


def partner(me, step, count):
    if count & (count - 1):
        return lax.rem(me + step, count)
    other, bit = 0, 1
    while bit < count:
        mine = lax.rem(me // bit, 2)
        other = other + bit * ((1 - mine) if step & bit else mine)
        bit *= 2
    return other


def source(me, step, count):
    if count & (count - 1):
        return lax.rem(me + count - step, count)
    return partner(me, step, count)


def as_row(col):
    n = col.shape[0]
    eye = lax.broadcasted_iota(jnp.int32, (n, n), 0) == lax.broadcasted_iota(jnp.int32, (n, n), 1)
    return jnp.sum(jnp.where(eye, col, 0), axis=0, keepdims=True)


def as_col(row):
    n = row.shape[1]
    eye = lax.broadcasted_iota(jnp.int32, (n, n), 0) == lax.broadcasted_iota(jnp.int32, (n, n), 1)
    return jnp.sum(jnp.where(eye, row, 0), axis=1, keepdims=True)


def kernel(
    nets,
    spans,
    buses,
    ptdf_hbm,
    demand,
    generation,
    cost,
    cap,
    storage,
    wear,
    initial,
    leakage,
    line_dual,
    line_index,
    rating,
    storage_bus,
    price_in,
    hour_block,
    block_price,
    gen_out,
    storage_out,
    charge_out,
    dual_out,
    price_out,
    ptdf,
    units,
    unit_cols,
    inj,
    acc,
    dual_half,
    part_send,
    part_recv,
    limit,
    sums,
    lasts,
    load_sem,
    unit_sem,
    inj_sem,
    part_sem,
    sum_sem,
    last_sem,
):
    f32, bf16 = jnp.float32, jnp.bfloat16
    me = lax.axis_index("net")
    place = lax.axis_index("tm")
    hours, nb = demand.shape
    rows = line_dual.shape[1]
    total_units = storage_bus.shape[1]
    su = storage.shape[1]

    def load(j):
        owner = source(me, j, nets)
        cols = pl.ds(pl.multiple_of(owner * nb, nb), nb)
        return pltpu.make_async_copy(ptdf_hbm.at[:, cols], ptdf.at[:, cols], load_sem.at[j])

    for j in range(nets):
        load(j).start()

    barrier = pltpu.get_barrier_semaphore()
    for step in range(1, nets):
        pl.semaphore_signal(
            barrier, inc=1, device_id={"net": partner(me, step, nets)}, device_id_type=MESH
        )
    for step in range(1, spans):
        pl.semaphore_signal(
            barrier, inc=1, device_id={"tm": lax.rem(place + step, spans)}, device_id_type=MESH
        )

    units[0] = storage[...].astype(bf16)
    inj[0, 0] = (generation[...] - demand[...]).astype(bf16)
    pl.semaphore_wait(barrier, nets - 1 + spans - 1)

    pending = []

    def send(src, dst, sems, step, axis="net"):
        if axis == "net":
            target = {"net": partner(me, step, nets)}
        else:
            target = {"tm": lax.rem(place + step, spans)}
        copy = pltpu.make_async_remote_copy(
            src_ref=src,
            dst_ref=dst,
            send_sem=sems.at[0, step],
            recv_sem=sems.at[1, step],
            device_id=target,
            device_id_type=MESH,
        )
        copy.start()
        pending.append(copy)
        return copy

    unit_copies = [send(units.at[0], units.at[s], unit_sem, s) for s in range(1, nets)]
    inj_copies = [send(inj.at[0, 0], inj.at[0, s], inj_sem.at[0], s) for s in range(1, nets)]

    index = line_index[...]
    lane, group = lax.rem(index, 128), index // 128
    found = jnp.zeros(index.shape, f32)
    for q in range(rating.shape[0]):
        row = jnp.broadcast_to(rating[q : q + 1, :], index.shape)
        found = jnp.where(
            group == q,
            jnp.take_along_axis(row, lane, axis=1, mode="promise_in_bounds"),
            found,
        )
    limit[...] = found

    unit_part = jnp.sum(storage[...], axis=1, keepdims=True)
    price = as_col(price_in[...])
    block = as_col(hour_block[...])
    kinds = block_price.shape[1]
    hour_price = jnp.sum(
        jnp.where(
            block == lax.broadcasted_iota(jnp.int32, (hours, kinds), 1), block_price[...], 0.0
        ),
        axis=1,
        keepdims=True,
    )

    for copy in unit_copies:
        copy.wait_recv()
    ub = min(256, nb)
    for j in range(nets):
        owner = source(me, j, nets)
        base = owner * nb

        def collect(i, c, j=j, base=base):
            bus = base + i * ub + lax.broadcasted_iota(jnp.int32, (ub, su), 0)
            total = jnp.zeros((hours, ub), f32)
            for k in range(nets):
                first = pl.multiple_of(source(me, k, nets) * su, su)
                hit = jnp.where(storage_bus[:, pl.ds(first, su)] == bus, 1.0, 0.0).astype(bf16)
                total = total + lax.dot_general(units[k], hit, NT, preferred_element_type=f32)
            high = total.astype(bf16)
            low = (total - high.astype(f32)).astype(bf16)
            unit_cols[j, :, pl.ds(pl.multiple_of(i * ub, ub), ub)] = jnp.concatenate(
                [high, low], axis=0
            )
            return c

        lax.fori_loop(0, nb // ub, collect, 0)

    rb = min(512, rows)
    cb = min(512, nb)
    gen = None
    for turn in range(PASSES):
        last_j = nets - 1
        for j in range(nets):
            if turn == 0:
                load(j).wait()
            if j > 0:
                inj_copies[j - 1].wait_recv()
            owner = source(me, j, nets)
            cols = pl.ds(pl.multiple_of(owner * nb, nb), nb)

            def flow(i, c, j=j, cols=cols):
                r = pl.ds(pl.multiple_of(i * rb, rb), rb)
                if turn == 0:
                    left = jnp.concatenate([inj[turn, j], unit_cols[j]], axis=0)
                    got = lax.dot_general(left, ptdf[r, cols], NT, preferred_element_type=f32)
                    unit = got[hours : 2 * hours] + got[2 * hours :]
                    got = got[:hours] + unit
                    if j == 0:
                        acc[1, :, r] = unit
                    else:
                        acc[1, :, r] = acc[1, :, r] + unit
                    old = line_dual
                else:
                    got = lax.dot_general(
                        inj[turn, j], ptdf[r, cols], NT, preferred_element_type=f32
                    )
                    if j == 0:
                        got = got + acc[1, :, r]
                    old = dual_out
                if j > 0:
                    got = got + acc[0, :, r]
                if j < last_j:
                    acc[0, :, r] = got
                else:
                    shifted = got + old[:, r]
                    pieces = []
                    for k in range(rb // 128):
                        bound = limit[pl.ds(i * (rb // 128) + k, 1), :]
                        x = shifted[:, k * 128 : (k + 1) * 128]
                        pieces.append(x - jnp.clip(x, -bound, bound))
                    dual = jnp.concatenate(pieces, axis=1)
                    dual_out[:, r] = dual
                    dual_half[:, r] = dual.astype(bf16)
                return c

            lax.fori_loop(0, rows // rb, flow, 0)

        part_copies = []
        for j in list(range(nets - 1, 0, -1)) + [0]:
            owner = partner(me, j, nets)

            def pull_part(i, c, j=j, owner=owner):
                here = pl.ds(pl.multiple_of(i * cb, cb), cb)
                cols = pl.ds(pl.multiple_of(owner * nb + i * cb, cb), cb)
                got = lax.dot_general(
                    dual_half[...], ptdf[:, cols], NN, preferred_element_type=f32
                )
                if j > 0:
                    part_send[turn, j, :, here] = got.astype(bf16)
                else:
                    acc[0, :, here] = got
                return c

            lax.fori_loop(0, nb // cb, pull_part, 0)
            if j > 0:
                part_copies.append(
                    send(part_send.at[turn, j], part_recv.at[turn, j], part_sem.at[turn], j)
                )
        pull = acc[0, :, :nb]
        for step in range(nets - 1, 0, -1):
            part_copies[nets - 1 - step].wait_recv()
            pull = pull + part_recv[turn, step].astype(f32)
        if turn == 0:
            gen = generation[...]
        else:
            gen = gen_out[...]
        trial = jnp.clip(gen - STEP * (cost[...] - price + pull), 0.0, cap[...])
        part = jnp.sum(trial - demand[...], axis=1, keepdims=True) + unit_part
        sums[turn, 0, :, :hours] = jnp.broadcast_to(as_row(part), (8, hours))
        sum_copies = [
            send(sums.at[turn, 0], sums.at[turn, s], sum_sem.at[turn], s) for s in range(1, nets)
        ]
        whole = sums[turn, 0]
        for s in range(1, nets):
            sum_copies[s - 1].wait_recv()
            whole = whole + sums[turn, s]
        mismatch = as_col(whole[0:1, :hours])
        gen = trial - mismatch / buses
        price = price - BAL * mismatch / buses
        gen_out[...] = gen
        if turn + 1 < PASSES:
            inj[turn + 1, 0] = (gen - demand[...]).astype(bf16)
            inj_copies = [
                send(inj.at[turn + 1, 0], inj.at[turn + 1, s], inj_sem.at[turn + 1], s)
                for s in range(1, nets)
            ]

    stored = storage[...]
    stored = jnp.clip(
        stored + STEP_UNIT * (price + hour_price - wear[...] * stored), -1.0, 1.0
    )
    storage_out[...] = stored
    keep = 1.0 - leakage[...]
    running = -ETA * stored
    hour = lax.broadcasted_iota(jnp.int32, (hours, su), 0)
    growth = jnp.ones((hours, su), f32)
    factor = keep
    span = 1
    while span < hours:
        moved = jnp.where(hour >= span, pltpu.roll(running, span, axis=0), 0.0)
        running = running + factor * moved
        growth = jnp.where(lax.rem((hour + 1) // span, 2) == 1, growth * factor, growth)
        factor = factor * factor
        span = span * 2
    while span <= hours:
        growth = jnp.where(lax.rem((hour + 1) // span, 2) == 1, growth * factor, growth)
        factor = factor * factor
        span = span * 2
    lasts[0] = jnp.broadcast_to(running[hours - 1 :, :], (8, su))
    last_copies = [
        send(lasts.at[0], lasts.at[s], last_sem, s, "tm") for s in range(1, spans)
    ]
    price_out[...] = as_row(price)
    block_keep = growth[hours - 1 :, :]
    for copy in last_copies:
        copy.wait_recv()
    entering = initial[...]
    for s in range(spans - 1, 0, -1):
        entering = jnp.where(s <= place, block_keep * entering + lasts[s, 0:1, :], entering)
    charge_out[...] = growth * entering + running
    for copy in pending:
        copy.wait_send()


def per_device(
    ptdf,
    demand,
    generation,
    cost,
    gen_cap,
    storage,
    wear,
    initial_charge,
    leakage,
    line_dual,
    line_index,
    rating,
    storage_bus,
    balance_dual,
    hour_block,
    block_price,
):
    nets, spans = lax.axis_size("net"), lax.axis_size("tm")
    rows, _ = ptdf.shape
    nb, hours = demand.shape
    su = storage.shape[0]
    buses = nb * nets
    f32, bf16 = jnp.float32, jnp.bfloat16
    vmem = pl.BlockSpec(memory_space=pltpu.VMEM)
    sem = pltpu.SemaphoreType.DMA
    gen, stored, charge, dual, price = pl.pallas_call(
        functools.partial(kernel, nets, spans, buses),
        out_shape=(
            jax.ShapeDtypeStruct((hours, nb), f32),
            jax.ShapeDtypeStruct((hours, su), f32),
            jax.ShapeDtypeStruct((hours, su), f32),
            jax.ShapeDtypeStruct((hours, rows), f32),
            jax.ShapeDtypeStruct((1, hours), f32),
        ),
        in_specs=[pl.BlockSpec(memory_space=pl.ANY)] + [vmem] * 15,
        out_specs=(vmem,) * 5,
        scratch_shapes=[
            pltpu.VMEM(ptdf.shape, bf16),
            pltpu.VMEM((nets, hours, su), bf16),
            pltpu.VMEM((nets, 2 * hours, nb), bf16),
            pltpu.VMEM((PASSES, nets, hours, nb), bf16),
            pltpu.VMEM((2, hours, max(rows, nb)), f32),
            pltpu.VMEM((hours, rows), bf16),
            pltpu.VMEM((PASSES, nets, hours, nb), bf16),
            pltpu.VMEM((PASSES, nets, hours, nb), bf16),
            pltpu.VMEM((rows // 128, 128), f32),
            pltpu.VMEM((PASSES, nets, 8, 128), f32),
            pltpu.VMEM((spans, 8, su), f32),
            sem((nets,)),
            sem((2, nets)),
            sem((PASSES, 2, nets)),
            sem((PASSES, 2, nets)),
            sem((PASSES, 2, nets)),
            sem((2, spans)),
        ],
        compiler_params=pltpu.CompilerParams(
            collective_id=0, has_side_effects=True, vmem_limit_bytes=64 * 1000 * 1000
        ),
    )(
        ptdf,
        demand.T,
        generation.T,
        cost.T,
        gen_cap[None, :],
        storage.T,
        wear[None, :],
        initial_charge[None, :],
        leakage[None, :],
        line_dual.T,
        line_index.reshape(-1, 128),
        rating.reshape(-1, 128),
        storage_bus[None, :],
        balance_dual[None, :],
        hour_block[None, :],
        block_price[None, :],
    )
    return (gen.T, stored.T, charge.T, dual.T, price[0])


def solution(mesh):
    in_specs = (
        P("net", None),
        P("net", "tm"),
        P("net", "tm"),
        P("net", "tm"),
        P("net"),
        P("net", "tm"),
        P("net"),
        P("net"),
        P("net"),
        P("net", "tm"),
        P("net"),
        P(),
        P(),
        P("tm"),
        P("tm"),
        P(),
    )
    out_specs = (P("net", "tm"), P("net", "tm"), P("net", "tm"), P("net", "tm"), P("tm"))
    return jax.shard_map(
        per_device, mesh=mesh, in_specs=in_specs, out_specs=out_specs, check_vma=False
    )
```

time: 339 us -> 91.1 us (0.27)
  local copies, waits for them, and re-layouts: 132 us -> 8.26 us
  Pallas kernels: 0 us -> 82 us
  blocking collectives: 74.3 us -> 0 us
  matrix products: 68.4 us -> 0 us
  waiting for transfers between devices: 36.4 us -> 0 us
  between operations: 14.6 us -> 0.65 us
  other arithmetic: 10.3 us -> 0 us
    gather x2 -> x0, local copies, waits for them, and re-layouts: 89.3 us -> none  [the longest x1 66.3 us: per_device(): unit_columns = jnp.take(ptdf, storage_bus, axis=1)]
    pallas_call x0 -> x1, Pallas kernels: none -> 82 us  [per_device(): pl.pallas_call(functools.partial(kernel, nets, spans, buses), out_shape=(...]
    dot_general x5 -> x0, matrix products: 68.4 us -> none  [the longest x2 31.6 us: per_device(): jnp.dot(ptdf, lax.all_gather(injection, 'net', axis=0, tiled=True), prefe...]
    all_gather x5 -> x0, blocking collectives: 56.4 us -> none  [the longest x2 25.6 us: prefix(): gathered = jax.tree.map(lambda a: lax.all_gather(a, axis), part)]
    reduce_scatter x2 -> x0, waiting for transfers between devices: 36.3 us -> none  [per_device(): lax.psum_scatter(lax.dot_general(ptdf, dual_half, (((0,), (0,)), ((), ())...]
    unnamed x57 -> x5, local copies, waits for them, and re-layouts: 41.8 us -> 8.26 us
    psum x2 -> x0, blocking collectives: 17.9 us -> none  [per_device(): lax.psum((jnp.sum(trial - demand, axis=0), unit_part), 'net')]
    reduce_sum x4 -> x0, other arithmetic: 3.5 us -> none  [the longest x2 2.31 us: per_device(): jnp.sum(trial - demand, axis=0)]
  transfers between devices with their start and end apart: 2 -> 0, of which waited for: 2 -> 0; matrix products, arithmetic and copies ran while one was open for 0% -> 0% of each run, Pallas kernels for 0% -> 0%
where the time goes in v1:
time: 91.1 us; the launch traced here: 90.9 us
  Pallas kernels  82 us (90%)
  local copies, waits for them, and re-layouts  8.26 us (9%)
    pallas_call x1, Pallas kernels, per_device(): pl.pallas_call(functools.partial(kernel, nets, spans, buses), out_shape=(...  82 us
    unnamed x5, local copies, waits for them, and re-layouts  8.26 us

profile of v1, /device:TPU:0, one launch (start us, length us, event | category | flops | bytes accessed | tf_op | source)
XLA Modules:
  0.0 90.9 jit_solution(12978404744876986065)
XLA Ops:
  0.6 82.0 %shard_map.191 = (f32[64,1024]{1,0:T(8,128)}, f32[64,512]{1,0:T(8,128)}, f32[64,512]{1,0:T(8,128)}, f32[64,4096]{1,0:T(8,128)}, f32[1,64]{1,0:T(1,128)}) custom-call(bf16[4096,4096]{1,0:T(8,128)(2,1)} %ptdf_hbm.1, f32[64,1024]{1,0:T(8,128)} %bitcast.22, f32[64,1024]{1,0:T(8,128)} %bitcast.23, f32[64,1024]{1,0:T(8,128)} %bitcast.24, f32[1,1024]{1,0:T(1,128)} %bitcast.32, ...), custom_call_target="tpu_custom_call" | custom-call | tf_op jit(solution)/shard_map/pallas_call | solution.py:354
  82.6 1.7 %copy.26 = f32[1024,64]{0,1:T(8,128)} copy(f32[1024,64]{0,1:T(8,128)} %bitcast.25) | data formatting | bytes 524288
  84.3 1.6 %copy.27 = f32[512,64]{0,1:T(8,128)} copy(f32[512,64]{0,1:T(8,128)} %bitcast.28) | data formatting | bytes 262144
  85.8 1.6 %copy.28 = f32[512,64]{0,1:T(8,128)} copy(f32[512,64]{0,1:T(8,128)} %bitcast.27) | data formatting | bytes 262144
  87.4 2.3 %copy.29 = f32[4096,64]{0,1:T(8,128)} copy(f32[4096,64]{0,1:T(8,128)} %bitcast.21) | data formatting | bytes 2097152
  89.7 1.2 %copy.30 = f32[64]{0:T(128)} copy(f32[64]{0:T(128)} %bitcast.39) | data formatting | bytes 512

commit v2 on v1

v2 whole, which is shorter than its diff:
```python
import functools

import jax
import jax.numpy as jnp
from jax import lax
from jax.experimental import pallas as pl
from jax.experimental.pallas import tpu as pltpu
from jax.sharding import PartitionSpec as P

PASSES = 2
STEP = 0.1
BAL = 0.5
STEP_UNIT = 0.2
ETA = 0.0625
MESH = pl.DeviceIdType.MESH
NT = (((1,), (1,)), ((), ()))
NN = (((1,), (0,)), ((), ()))


def peer(me, step, count):
    other, bit = 0, 1
    while bit < count:
        mine = lax.rem(me // bit, 2)
        other = other + bit * ((1 - mine) if step & bit else mine)
        bit *= 2
    return other


def as_row(col):
    n = col.shape[0]
    eye = lax.broadcasted_iota(jnp.int32, (n, n), 0) == lax.broadcasted_iota(jnp.int32, (n, n), 1)
    return jnp.sum(jnp.where(eye, col, 0), axis=0, keepdims=True)


def as_col(row):
    n = row.shape[1]
    eye = lax.broadcasted_iota(jnp.int32, (n, n), 0) == lax.broadcasted_iota(jnp.int32, (n, n), 1)
    return jnp.sum(jnp.where(eye, row, 0), axis=1, keepdims=True)


def kernel(
    nets,
    spans,
    buses,
    groups,
    ptdf_hbm,
    line_dual_hbm,
    cost_hbm,
    demand,
    generation,
    cap,
    storage,
    wear,
    initial,
    leakage,
    line_index,
    rating,
    storage_bus,
    price_in,
    hour_block,
    block_price,
    gen_out,
    storage_out,
    charge_out,
    dual_out,
    price_out,
    ptdf,
    line_dual,
    cost,
    units,
    unit_cols,
    inj,
    inj_other,
    acc,
    pull_own,
    flow_send,
    flow_recv,
    dual_half,
    part_send,
    part_recv,
    limit,
    sums,
    lasts,
    load_sem,
    unit_sem,
    inj_sem,
    part_sem,
    flow_sem,
    dual_sem,
    sum_sem,
    last_sem,
):
    f32, bf16 = jnp.float32, jnp.bfloat16
    me = lax.axis_index("net")
    place = lax.axis_index("tm")
    core = lax.rem(place, 2)
    twin = place + 1 - 2 * core
    hours, nb = demand.shape
    hb = nb // 2
    rows = ptdf.shape[1]
    su = storage.shape[1]
    halves = [
        pl.ds(pl.multiple_of(core * hb, hb), hb),
        pl.ds(pl.multiple_of((1 - core) * hb, hb), hb),
    ]

    def load(j):
        first = pl.multiple_of(peer(me, j, nets) * nb + core * hb, hb)
        return pltpu.make_async_copy(ptdf_hbm.at[:, pl.ds(first, hb)], ptdf.at[j], load_sem.at[j])

    load_dual = pltpu.make_async_copy(line_dual_hbm, line_dual, load_sem.at[nets])
    load_cost = pltpu.make_async_copy(cost_hbm, cost, load_sem.at[nets + 1])
    for j in range(nets):
        load(j).start()
    load_dual.start()
    load_cost.start()

    def device(j, across):
        return {"net": peer(me, j, nets), "tm": twin if across else place}

    barrier = pltpu.get_barrier_semaphore()
    for j in range(1, nets):
        for across in (0, 1):
            pl.semaphore_signal(
                barrier, inc=1, device_id=device(j, across), device_id_type=MESH
            )
    for step in range(1, spans):
        pl.semaphore_signal(
            barrier, inc=1, device_id={"tm": lax.rem(place + step, spans)}, device_id_type=MESH
        )

    units[0, :hours] = storage[...].astype(bf16)
    for h in range(2):
        mine = (generation[:, halves[h]] - demand[:, halves[h]]).astype(bf16)
        if h == 0:
            inj[0, 0, :hours] = mine
        else:
            inj_other[0] = mine
    pl.semaphore_wait(barrier, 2 * (nets - 1) + spans - 1)

    pending = []

    def send(src, dst, sems, slot, target):
        copy = pltpu.make_async_remote_copy(
            src_ref=src,
            dst_ref=dst,
            send_sem=sems.at[0, slot],
            recv_sem=sems.at[1, slot],
            device_id=target,
            device_id_type=MESH,
        )
        copy.start()
        pending.append(copy)
        return copy

    own, other = pl.ds(0, hours), pl.ds(hours, hours)

    def send_injection(turn):
        copies = {}
        copies[0, 1] = send(
            inj_other.at[turn], inj.at[turn, 0, other], inj_sem.at[turn], 1, device(0, 1)
        )
        for j in range(1, nets):
            copies[j, 0] = send(
                inj.at[turn, 0, own], inj.at[turn, j, own], inj_sem.at[turn], 2 * j, device(j, 0)
            )
            copies[j, 1] = send(
                inj_other.at[turn],
                inj.at[turn, j, other],
                inj_sem.at[turn],
                2 * j + 1,
                device(j, 1),
            )
        return copies

    unit_copies = [
        send(units.at[0, own], units.at[j, own], unit_sem, 2 * j, device(j, 0))
        for j in range(1, nets)
    ]
    passed_on = [send(units.at[0, own], units.at[0, other], unit_sem, 1, device(0, 1))]
    inj_copies = send_injection(0)

    index = line_index[...]
    lane, group = lax.rem(index, 128), index // 128
    found = jnp.zeros(index.shape, f32)
    for q in range(rating.shape[0]):
        row = jnp.broadcast_to(rating[q : q + 1, :], index.shape)
        found = jnp.where(
            group == q,
            jnp.take_along_axis(row, lane, axis=1, mode="promise_in_bounds"),
            found,
        )
    limit[...] = found

    unit_part = jnp.sum(storage[...], axis=1, keepdims=True)
    price = as_col(price_in[...])
    block = as_col(hour_block[...])
    kinds = block_price.shape[1]
    hour_price = jnp.sum(
        jnp.where(
            block == lax.broadcasted_iota(jnp.int32, (hours, kinds), 1), block_price[...], 0.0
        ),
        axis=1,
        keepdims=True,
    )

    for j in range(1, nets):
        unit_copies[j - 1].wait_recv()
        passed_on.append(
            send(units.at[j, own], units.at[j, other], unit_sem, 2 * j + 1, device(0, 1))
        )
    for copy in passed_on:
        copy.wait_recv()
    ub = min(256, hb)
    for j in range(nets):
        base = peer(me, j, nets) * nb + core * hb

        def collect(i, c, j=j, base=base):
            bus = base + i * ub + lax.broadcasted_iota(jnp.int32, (ub, su), 0)
            total = jnp.zeros((2 * hours, ub), f32)
            for k in range(nets):
                first = pl.multiple_of(peer(me, k, nets) * su, su)
                hit = jnp.where(storage_bus[:, pl.ds(first, su)] == bus, 1.0, 0.0).astype(bf16)
                total = total + lax.dot_general(units[k], hit, NT, preferred_element_type=f32)
            unit_cols[j, :, pl.ds(pl.multiple_of(i * ub, ub), ub)] = total.astype(bf16)
            return c

        lax.fori_loop(0, hb // ub, collect, 0)

    span_rows = rows // groups
    rb = min(512, span_rows)
    cb = min(512, hb)
    load_dual.wait()
    for turn in range(PASSES):
        old = line_dual if turn == 0 else dual_out
        flow_copies, dual_copies = [], []

        def settle(g):
            flow_copies[g].wait_recv()
            for k in range(span_rows // 128):
                i = g * (span_rows // 128) + k
                r = pl.ds(i * 128, 128)
                bound = limit[i : i + 1, :]
                x = acc[0, :hours, r] + flow_recv[turn, :, r] + old[:, r]
                dual = x - jnp.clip(x, -bound, bound)
                dual_out[:, r] = dual
                dual_half[turn, :hours, r] = dual.astype(bf16)
            r = pl.ds(g * span_rows, span_rows)
            dual_copies.append(
                send(
                    dual_half.at[turn, own, r],
                    dual_half.at[turn, other, r],
                    dual_sem.at[turn],
                    g,
                    device(0, 1),
                )
            )

        for j in range(nets):
            last = j == nets - 1
            if turn == 0:
                load(j).wait()
            if j > 0:
                inj_copies[j, 0].wait_recv()
            inj_copies[j, 1].wait_recv()

            def flow(i, c, j=j, last=last):
                r = pl.ds(pl.multiple_of(i * rb, rb), rb)
                if turn == 0:
                    left = jnp.concatenate([inj[turn, j], unit_cols[j]], axis=0)
                    got = lax.dot_general(left, ptdf[j, r, :], NT, preferred_element_type=f32)
                    unit = got[2 * hours :]
                    got = got[: 2 * hours] + unit
                    if j > 0:
                        unit = unit + acc[1, :, r]
                    acc[1, :, r] = unit
                else:
                    got = lax.dot_general(
                        inj[turn, j], ptdf[j, r, :], NT, preferred_element_type=f32
                    )
                    if j == 0:
                        got = got + acc[1, :, r]
                if j > 0:
                    got = got + acc[0, :, r]
                if last:
                    acc[0, :hours, r] = got[:hours]
                    flow_send[turn, :, r] = got[hours:]
                else:
                    acc[0, :, r] = got
                return c

            if not last:
                lax.fori_loop(0, rows // rb, flow, 0)
        per_group = span_rows // rb
        for g in range(groups + 2):
            if g < groups:
                lax.fori_loop(g * per_group, (g + 1) * per_group, flow, 0)
                r = pl.ds(g * span_rows, span_rows)
                flow_copies.append(
                    send(
                        flow_send.at[turn, :, r],
                        flow_recv.at[turn, :, r],
                        flow_sem.at[turn],
                        g,
                        device(0, 1),
                    )
                )
            if g >= 2:
                settle(g - 2)
        for copy in dual_copies:
            copy.wait_recv()

        part_copies = {}
        for j in list(range(nets - 1, -1, -1)):

            def pull_part(i, c, j=j):
                here = pl.ds(pl.multiple_of(i * cb, cb), cb)
                got = lax.dot_general(
                    dual_half[turn], ptdf[j, :, here], NN, preferred_element_type=f32
                )
                if j > 0:
                    part_send[turn, j, :, here] = got.astype(bf16)
                else:
                    pull_own[:, here] = got[:hours]
                    part_send[turn, j, other, here] = got[hours:].astype(bf16)
                return c

            lax.fori_loop(0, hb // cb, pull_part, 0)
            for h, side in enumerate((own, other)):
                if j or h:
                    part_copies[j, h] = send(
                        part_send.at[turn, j, side],
                        part_recv.at[turn, j, side],
                        part_sem.at[turn],
                        2 * j + h,
                        device(j, h),
                    )
        if turn == 0:
            load_cost.wait()
        gen_old = generation if turn == 0 else gen_out
        part = unit_part
        for j in range(nets - 1, -1, -1):
            for h in range(2):
                if j or h:
                    part_copies[j, h].wait_recv()
        for h, side in enumerate((own, other)):
            pull = pull_own[...] if h == 0 else part_recv[turn, 0, side].astype(f32)
            for j in range(1, nets):
                pull = pull + part_recv[turn, j, side].astype(f32)
            cols = halves[h]
            trial = jnp.clip(
                gen_old[:, cols] - STEP * (cost[:, cols] - price + pull), 0.0, cap[:, cols]
            )
            gen_out[:, cols] = trial
            part = part + jnp.sum(trial - demand[:, cols], axis=1, keepdims=True)
        sums[turn, 0, :, :hours] = jnp.broadcast_to(as_row(part), (8, hours))
        sum_copies = [
            send(sums.at[turn, 0], sums.at[turn, j], sum_sem.at[turn], j, device(j, 0))
            for j in range(1, nets)
        ]
        whole = sums[turn, 0]
        for j in range(1, nets):
            sum_copies[j - 1].wait_recv()
            whole = whole + sums[turn, j]
        mismatch = as_col(whole[0:1, :hours])
        price = price - BAL * mismatch / buses
        for h in range(2):
            gen = gen_out[:, halves[h]] - mismatch / buses
            gen_out[:, halves[h]] = gen
            if turn + 1 < PASSES:
                mine = (gen - demand[:, halves[h]]).astype(bf16)
                if h == 0:
                    inj[turn + 1, 0, :hours] = mine
                else:
                    inj_other[turn + 1] = mine
        if turn + 1 < PASSES:
            inj_copies = send_injection(turn + 1)

    stored = storage[...]
    stored = jnp.clip(
        stored + STEP_UNIT * (price + hour_price - wear[...] * stored), -1.0, 1.0
    )
    storage_out[...] = stored
    keep = 1.0 - leakage[...]
    running = -ETA * stored
    hour = lax.broadcasted_iota(jnp.int32, (hours, su), 0)
    growth = jnp.ones((hours, su), f32)
    factor = keep
    span = 1
    while span < hours:
        moved = jnp.where(hour >= span, pltpu.roll(running, span, axis=0), 0.0)
        running = running + factor * moved
        growth = jnp.where(lax.rem((hour + 1) // span, 2) == 1, growth * factor, growth)
        factor = factor * factor
        span = span * 2
    while span <= hours:
        growth = jnp.where(lax.rem((hour + 1) // span, 2) == 1, growth * factor, growth)
        factor = factor * factor
        span = span * 2
    lasts[0] = jnp.broadcast_to(running[hours - 1 :, :], (8, su))
    last_copies = [
        send(lasts.at[0], lasts.at[s], last_sem, s, {"tm": lax.rem(place + s, spans)})
        for s in range(1, spans)
    ]
    price_out[...] = as_row(price)
    block_keep = growth[hours - 1 :, :]
    for copy in last_copies:
        copy.wait_recv()
    entering = initial[...]
    for s in range(spans - 1, 0, -1):
        entering = jnp.where(s <= place, block_keep * entering + lasts[s, 0:1, :], entering)
    charge_out[...] = growth * entering + running
    for copy in pending:
        copy.wait_send()


def write_out(*refs):
    count = len(refs) // 2
    for source, target in zip(refs[:count], refs[count:]):
        target[...] = source[...]


def per_device(
    ptdf,
    demand,
    generation,
    cost,
    gen_cap,
    storage,
    wear,
    initial_charge,
    leakage,
    line_dual,
    line_index,
    rating,
    storage_bus,
    balance_dual,
    hour_block,
    block_price,
):
    nets, spans = lax.axis_size("net"), lax.axis_size("tm")
    rows, _ = ptdf.shape
    nb, hours = demand.shape
    su = storage.shape[0]
    buses, hb = nb * nets, nb // 2
    groups = 4 if rows % 512 == 0 else 1
    f32, bf16 = jnp.float32, jnp.bfloat16
    vmem = pl.BlockSpec(memory_space=pltpu.VMEM)
    hbm = pl.BlockSpec(memory_space=pl.ANY)
    sem = pltpu.SemaphoreType.DMA
    out_shape = (
        jax.ShapeDtypeStruct((hours, nb), f32),
        jax.ShapeDtypeStruct((hours, su), f32),
        jax.ShapeDtypeStruct((hours, su), f32),
        jax.ShapeDtypeStruct((hours, rows), f32),
        jax.ShapeDtypeStruct((1, hours), f32),
    )
    found = pl.pallas_call(
        functools.partial(kernel, nets, spans, buses, groups),
        out_shape=out_shape,
        in_specs=[hbm] * 3 + [vmem] * 13,
        out_specs=(vmem,) * 5,
        scratch_shapes=[
            pltpu.VMEM((nets, rows, hb), bf16),
            pltpu.VMEM((hours, rows), f32),
            pltpu.VMEM((hours, nb), f32),
            pltpu.VMEM((nets, 2 * hours, su), bf16),
            pltpu.VMEM((nets, 2 * hours, hb), bf16),
            pltpu.VMEM((PASSES, nets, 2 * hours, hb), bf16),
            pltpu.VMEM((PASSES, hours, hb), bf16),
            pltpu.VMEM((2, 2 * hours, rows), f32),
            pltpu.VMEM((hours, hb), f32),
            pltpu.VMEM((PASSES, hours, rows), f32),
            pltpu.VMEM((PASSES, hours, rows), f32),
            pltpu.VMEM((PASSES, 2 * hours, rows), bf16),
            pltpu.VMEM((PASSES, nets, 2 * hours, hb), bf16),
            pltpu.VMEM((PASSES, nets, 2 * hours, hb), bf16),
            pltpu.VMEM((rows // 128, 128), f32),
            pltpu.VMEM((PASSES, nets, 8, 128), f32),
            pltpu.VMEM((spans, 8, su), f32),
            sem((nets + 2,)),
            sem((2, 2 * nets)),
            sem((PASSES, 2, 2 * nets)),
            sem((PASSES, 2, 2 * nets)),
            sem((PASSES, 2, groups)),
            sem((PASSES, 2, groups)),
            sem((PASSES, 2, nets)),
            sem((2, spans)),
        ],
        compiler_params=pltpu.CompilerParams(
            collective_id=0, has_side_effects=True, vmem_limit_bytes=64 * 1000 * 1000
        ),
    )(
        ptdf,
        line_dual.T,
        cost.T,
        demand.T,
        generation.T,
        gen_cap[None, :],
        storage.T,
        wear[None, :],
        initial_charge[None, :],
        leakage[None, :],
        line_index.reshape(-1, 128),
        rating.reshape(-1, 128),
        storage_bus[None, :],
        balance_dual[None, :],
        hour_block[None, :],
        block_price[None, :],
    )
    gen, stored, charge, dual, price = pl.pallas_call(
        write_out,
        out_shape=out_shape,
        in_specs=[vmem] * 5,
        out_specs=(vmem,) * 5,
        compiler_params=pltpu.CompilerParams(vmem_limit_bytes=8 * 2**20),
    )(*found)
    return (gen.T, stored.T, charge.T, dual.T, price[0])


def solution(mesh):
    in_specs = (
        P("net", None),
        P("net", "tm"),
        P("net", "tm"),
        P("net", "tm"),
        P("net"),
        P("net", "tm"),
        P("net"),
        P("net"),
        P("net"),
        P("net", "tm"),
        P("net"),
        P(),
        P(),
        P("tm"),
        P("tm"),
        P(),
    )
    out_specs = (P("net", "tm"), P("net", "tm"), P("net", "tm"), P("net", "tm"), P("tm"))
    return jax.shard_map(
        per_device, mesh=mesh, in_specs=in_specs, out_specs=out_specs, check_vma=False
    )
```

time: 91.1 us -> 83.4 us (0.915)
  Pallas kernels: 82 us -> 77.8 us
  local copies, waits for them, and re-layouts: 8.26 us -> 4.64 us
    pallas_call x1 -> x2, Pallas kernels: 82 us -> 77.8 us  [the longest x1 76.6 us: per_device(): pl.pallas_call(functools.partial(kernel, nets, spans, buses, groups), out...]
    unnamed x5 -> x10, local copies, waits for them, and re-layouts: 8.26 us -> 4.64 us
where the time goes in v2:
time: 83.4 us; the launch traced here: 83.1 us
  Pallas kernels  77.8 us (93%)
  local copies, waits for them, and re-layouts  4.64 us (6%)
    pallas_call x1, Pallas kernels, per_device(): pl.pallas_call(functools.partial(kernel, nets, spans, buses, groups), out...  76.6 us
    unnamed x10, local copies, waits for them, and re-layouts  4.64 us

profile of v2, /device:TPU:0, one launch (start us, length us, event | category | flops | bytes accessed | tf_op | source)
XLA Modules:
  0.0 83.1 jit_solution(10705366288581944657)
XLA Ops:
  0.6 76.6 %shard_map.191 = (f32[64,1024]{1,0:T(8,128)}, f32[64,512]{1,0:T(8,128)}, f32[64,512]{1,0:T(8,128)}, f32[64,4096]{1,0:T(8,128)}, f32[1,64]{1,0:T(1,128)}) custom-call(bf16[4096,4096]{1,0:T(8,128)(2,1)} %ptdf_hbm.1, f32[64,4096]{1,0:T(8,128)} %bitcast.20, f32[64,1024]{1,0:T(8,128)} %bitcast.21, f32[64,1024]{1,0:T(8,128)} %bitcast.22, f32[64,1024]{1,0:T(8,128)} %bitcast.23, ...), custom_call_target="tpu_custom_call" | custom-call | tf_op jit(solution)/shard_map/pallas_call | solution.py:458
  77.2 0.0 copy-start
  77.2 1.2 %copy-done = f32[64,4096]{1,0:T(8,128)S(1)} copy-done((f32[64,4096]{1,0:T(8,128)S(1)}, f32[64,4096]{1,0:T(8,128)}, u32[]{:S(2)}) %copy-start) | copy-done | bytes 1048600
  78.5 0.0 copy-start.1
  78.5 0.9 %copy-done.1 = f32[64,1024]{1,0:T(8,128)S(1)} copy-done((f32[64,1024]{1,0:T(8,128)S(1)}, f32[64,1024]{1,0:T(8,128)}, u32[]{:S(2)}) %copy-start.1) | copy-done | bytes 262168
  79.4 0.0 copy-start.2
  79.4 0.9 %copy-done.2 = f32[64,512]{1,0:T(8,128)S(1)} copy-done((f32[64,512]{1,0:T(8,128)S(1)}, f32[64,512]{1,0:T(8,128)}, u32[]{:S(2)}) %copy-start.2) | copy-done | bytes 131096
  80.3 0.0 copy-start.3
  80.3 0.9 %copy-done.3 = f32[64,512]{1,0:T(8,128)S(1)} copy-done((f32[64,512]{1,0:T(8,128)S(1)}, f32[64,512]{1,0:T(8,128)}, u32[]{:S(2)}) %copy-start.3) | copy-done | bytes 131096
  81.2 0.0 copy-start.4
  81.2 0.7 copy-done.4
  81.9 1.2 %shard_map.192 = (f32[64,1024]{1,0:T(8,128)}, f32[64,512]{1,0:T(8,128)}, f32[64,512]{1,0:T(8,128)}, f32[64,4096]{1,0:T(8,128)}, f32[1,64]{1,0:T(1,128)}) custom-call(f32[64,1024]{1,0:T(8,128)S(1)} %copy-done.1, f32[64,512]{1,0:T(8,128)S(1)} %copy-done.2, f32[64,512]{1,0:T(8,128)S(1)} %copy-done.3, f32[64,4096]{1,0:T(8,128)S(1)} %copy-done, f32[1,64]{1,0:T(1,128)S(1)} %copy-done.4), custom_call_target="tpu_custom_call" | custom-call | tf_op jit(solution)/shard_map/pallas_call | solution.py:511
Async XLA Ops:
  77.2 1.2 %copy-start = (f32[64,4096]{1,0:T(8,128)S(1)}, f32[64,4096]{1,0:T(8,128)}, u32[]{:S(2)}) copy-start(f32[64,4096]{1,0:T(8,128)} %get-tuple-element.18.refs_3_) | copy-start | bytes 3145732
  78.5 0.9 %copy-start.1 = (f32[64,1024]{1,0:T(8,128)S(1)}, f32[64,1024]{1,0:T(8,128)}, u32[]{:S(2)}) copy-start(f32[64,1024]{1,0:T(8,128)} %get-tuple-element.15.refs_0_) | copy-start | bytes 786436
  79.4 0.9 %copy-start.2 = (f32[64,512]{1,0:T(8,128)S(1)}, f32[64,512]{1,0:T(8,128)}, u32[]{:S(2)}) copy-start(f32[64,512]{1,0:T(8,128)} %get-tuple-element.16.refs_1_) | copy-start | bytes 393220
  80.3 0.9 %copy-start.3 = (f32[64,512]{1,0:T(8,128)S(1)}, f32[64,512]{1,0:T(8,128)}, u32[]{:S(2)}) copy-start(f32[64,512]{1,0:T(8,128)} %get-tuple-element.17.refs_2_) | copy-start | bytes 393220
  81.2 0.7 copy-start.4

commit v3 on v2

--- a/solution.py
+++ b/solution.py
@@ -211,7 +211,7 @@
         )
     for copy in passed_on:
         copy.wait_recv()
-    ub = min(256, hb)
+    ub = min(512, hb)
     for j in range(nets):
         base = peer(me, j, nets) * nb + core * hb
 
@@ -228,7 +228,7 @@
         lax.fori_loop(0, hb // ub, collect, 0)
 
     span_rows = rows // groups
-    rb = min(512, span_rows)
+    rb = 2048 if rows % 2048 == 0 else span_rows
     cb = min(512, hb)
     load_dual.wait()
     for turn in range(PASSES):
@@ -265,7 +265,8 @@
             inj_copies[j, 1].wait_recv()
 
             def flow(i, c, j=j, last=last):
-                r = pl.ds(pl.multiple_of(i * rb, rb), rb)
+                size = span_rows if last else rb
+                r = pl.ds(pl.multiple_of(i * size, size), size)
                 if turn == 0:
                     left = jnp.concatenate([inj[turn, j], unit_cols[j]], axis=0)
                     got = lax.dot_general(left, ptdf[j, r, :], NT, preferred_element_type=f32)
@@ -291,10 +292,9 @@
 
             if not last:
                 lax.fori_loop(0, rows // rb, flow, 0)
-        per_group = span_rows // rb
         for g in range(groups + 2):
             if g < groups:
-                lax.fori_loop(g * per_group, (g + 1) * per_group, flow, 0)
+                lax.fori_loop(g, g + 1, flow, 0)
                 r = pl.ds(g * span_rows, span_rows)
                 flow_copies.append(
                     send(
@@ -513,7 +513,7 @@
         out_shape=out_shape,
         in_specs=[vmem] * 5,
         out_specs=(vmem,) * 5,
-        compiler_params=pltpu.CompilerParams(vmem_limit_bytes=8 * 2**20),
+        compiler_params=pltpu.CompilerParams(vmem_limit_bytes=64 * 1000 * 1000),
     )(*found)
     return (gen.T, stored.T, charge.T, dual.T, price[0])
 

time: 83.4 us -> 72.2 us (0.87)
  Pallas kernels: 77.8 us -> 71.4 us
  local copies, waits for them, and re-layouts: 4.64 us -> 0 us
    pallas_call x1, Pallas kernels: 76.6 us -> 68.9 us  [per_device(): pl.pallas_call(functools.partial(kernel, nets, spans, buses, groups), out...]
    unnamed x10 -> x0, local copies, waits for them, and re-layouts: 4.64 us -> none
    pallas_call x1, Pallas kernels: 1.23 us -> 2.54 us  [per_device(): pl.pallas_call(write_out, out_shape=out_shape, in_specs=[vmem] * 5, out_s...]
where the time goes in v3:
time: 72.2 us; the launch traced here: 72.1 us
  Pallas kernels  71.4 us (99%)
    pallas_call x1, Pallas kernels, per_device(): pl.pallas_call(functools.partial(kernel, nets, spans, buses, groups), out...  68.9 us
    pallas_call x1, Pallas kernels, per_device(): pl.pallas_call(write_out, out_shape=out_shape, in_specs=[vmem] * 5, out_s...  2.54 us

profile of v3, /device:TPU:0, one launch (start us, length us, event | category | flops | bytes accessed | tf_op | source)
XLA Modules:
  0.0 72.1 jit_solution(14306137485340780743)
XLA Ops:
  0.6 68.9 %shard_map.191 = (f32[64,1024]{1,0:T(8,128)}, f32[64,512]{1,0:T(8,128)}, f32[64,512]{1,0:T(8,128)}, f32[64,4096]{1,0:T(8,128)}, f32[1,64]{1,0:T(1,128)}) custom-call(bf16[4096,4096]{1,0:T(8,128)(2,1)} %ptdf_hbm.1, f32[64,4096]{1,0:T(8,128)} %bitcast.20, f32[64,1024]{1,0:T(8,128)} %bitcast.21, f32[64,1024]{1,0:T(8,128)} %bitcast.22, f32[64,1024]{1,0:T(8,128)} %bitcast.23, ...), custom_call_target="tpu_custom_call" | custom-call | tf_op jit(solution)/shard_map/pallas_call | solution.py:458
  69.5 2.5 %shard_map.192 = (f32[64,1024]{1,0:T(8,128)}, f32[64,512]{1,0:T(8,128)}, f32[64,512]{1,0:T(8,128)}, f32[64,4096]{1,0:T(8,128)}, f32[1,64]{1,0:T(1,128)}) custom-call(f32[64,1024]{1,0:T(8,128)} %get-tuple-element.15.refs_0_, f32[64,512]{1,0:T(8,128)} %get-tuple-element.16.refs_1_, f32[64,512]{1,0:T(8,128)} %get-tuple-element.17.refs_2_, ...), custom_call_target="tpu_custom_call" | custom-call | tf_op jit(solution)/shard_map/pallas_call | solution.py:511
